TPU v7x, 32 devices: a whole 2x2x4 slice. The times are simulated.
32 devices in a mesh: groups: 2 (over y), tm: 4 (over z), batch: 2 (over x), rep: 2 (over core).
Axes of the slice: x: 2, y: 2, z: 4, core: 2. Of those that a mesh axis runs over, the one named last changes fastest.
Arguments:
- latents: bfloat16 [8, 2048, 512], P(('groups', 'batch', 'rep'), 'tm'), parts along dimension 0, may hold values from -6 to 6
- session_ids: int32 [8], P(('groups', 'batch', 'rep')), parts along dimension 0, may hold values from 0 to 7
- session_gain: float32 [8, 512], replicated, may hold values from 0.25 to 1.75
- session_shift: float32 [8, 512], replicated, may hold values from -3 to 3
- first_conv_weight: bfloat16 [3, 512, 512], replicated, may hold values from -0.15625 to 0.15625
- first_conv_bias: float32 [512], replicated, may hold values from -1.5 to 1.5
- second_conv_weight: bfloat16 [3, 512, 512], replicated, may hold values from -0.15625 to 0.15625
- second_conv_bias: float32 [512], replicated, may hold values from -1.5 to 1.5
- proj_weight: bfloat16 [512, 128], replicated, may hold values from -0.25 to 0.25
- offsets: int32 [8, 2048], P(('groups', 'batch', 'rep'), 'tm'), parts along dimension 0, may hold values from 1 to 10
- counts: int32 [8, 4], P(('groups', 'batch', 'rep'), 'tm'), parts along dimension 0, may hold values from 128 to 512, as said below
Outputs:
- embedding: bfloat16 [8, 2048, 128], P(('groups', 'batch', 'rep'), 'tm'), parts along dimension 0
- grad_conv: float32 [6, 512, 512], P('groups', None, 'tm'), parts along dimension 0
- grad_bias: float32 [1024], P(('groups', 'tm')), parts along dimension 0
- grad_proj: float32 [1024, 128], P(('groups', 'tm')), parts along dimension 0
There are 2 independent parts, one for each index of `groups`. A program takes and returns all parts, laid end to end along the dimension named above; an argument that names none is the same for every part. Nothing has to cross between parts.
Inputs may be any that keep to these rules, and one draw needn't show every extreme that they name: `counts`: bin t of a slab is live when t is below the slab's count.
All inputs are finite; a program needn't handle non-finite values.
Results may differ from a plain program's by a relative error of at most 0.0063.
Values may be sent and summed in bfloat16 or wider, within the bound.
A program may use at most 64 MiB of HBM per device.

v0:
```python
import jax
import jax.numpy as jnp
from jax import lax
from jax.sharding import PartitionSpec as P

FIRST_DILATION = 1
SECOND_DILATION = 2
OFF_MAX = 10


reciprocal_softness = 2.0


def padded_2(block, sides, width):
    for axis, dim in sides:
        count = lax.axis_size(axis)
        forward = [(i, i + 1) for i in range(count - 1)]
        backward = [(target, source) for source, target in forward]
        low = lax.ppermute(
            lax.slice_in_dim(block, block.shape[dim] - width, None, axis=dim), axis, forward
        )
        high = lax.ppermute(lax.slice_in_dim(block, 0, width, axis=dim), axis, backward)
        block = jnp.concatenate([low, block, high], axis=dim)
    return block


def passed_along(value, axis, steps):
    count = lax.axis_size(axis)
    leading, last = (max(0, -steps), min(count, count - steps))
    return lax.ppermute(value, axis, [(source, source + steps) for source in range(leading, last)])


def convolved_rows(padded, couple_coefficient, bias, dilation, count):
    total = jnp.zeros((count, couple_coefficient.shape[2]), jnp.float32) + bias[None, :]
    for filter_tap_index in range(3):
        shifted = padded[filter_tap_index * dilation : filter_tap_index * dilation + count]
        total = total + jnp.dot(
            shifted, couple_coefficient[filter_tap_index], preferred_element_type=jnp.float32
        )
    return total


def pair_weights(embed, piece_embed, portion_valid, own_first):
    cosine_affinity_matrix = reciprocal_softness * lax.dot_general(
        embed, piece_embed, (((1,), (1,)), ((), ())), preferred_element_type=jnp.float32
    )
    local_embedding = own_first + jnp.arange(embed.shape[0])[:, None]
    remote_embedding = jnp.arange(piece_embed.shape[0])[None, :]
    return (
        jnp.where(
            local_embedding != remote_embedding,
            jnp.exp(cosine_affinity_matrix - reciprocal_softness),
            0.0,
        )
        * portion_valid[None, :]
    )


def per_device(
    latents,
    session_ids,
    session_gain,
    session_shift,
    first_conv_weight,
    first_conv_bias,
    second_conv_weight,
    second_conv_bias,
    proj_weight,
    offsets,
    counts,
):
    count_of_rows = latents.shape[1]
    channels = latents.shape[2]
    slab_index = lax.axis_index("tm")
    slab_count = lax.axis_size("tm")
    picker = (session_ids[:, None] == jnp.arange(session_gain.shape[0])[None, :]).astype(
        jnp.float32
    )
    gain_row = jnp.dot(picker, session_gain, precision=lax.Precision.HIGHEST)
    shift_row = jnp.dot(picker, session_shift, precision=lax.Precision.HIGHEST)
    base_offset = (latents[0].astype(jnp.float32) * gain_row + shift_row).astype(jnp.bfloat16)
    input_padded = padded_2(base_offset, (("tm", 0),), FIRST_DILATION)
    first_preactivation = convolved_rows(
        input_padded, first_conv_weight, first_conv_bias, FIRST_DILATION, count_of_rows
    )
    first_hidden = (base_offset.astype(jnp.float32) + jax.nn.gelu(first_preactivation)).astype(
        jnp.bfloat16
    )
    first_padded = padded_2(first_hidden, (("tm", 0),), SECOND_DILATION)
    second_preactivation = convolved_rows(
        first_padded, second_conv_weight, second_conv_bias, SECOND_DILATION, count_of_rows
    )
    hidden_two = (first_hidden.astype(jnp.float32) + jax.nn.gelu(second_preactivation)).astype(
        jnp.bfloat16
    )
    feats = jnp.dot(hidden_two, proj_weight, preferred_element_type=jnp.float32)
    scale = lax.rsqrt(jnp.sum(feats * feats, axis=1) + 1e-06)
    unit = feats * scale[:, None]
    embed = unit.astype(jnp.bfloat16)
    usable_mask_vector = (jnp.arange(count_of_rows) < counts[0, 0]).astype(jnp.float32)
    live_flags = usable_mask_vector.astype(jnp.bfloat16)
    earlier = passed_along(embed[count_of_rows - OFF_MAX :], "tm", 1)
    extended = jnp.concatenate([earlier, embed], axis=0)
    slab_first = slab_index * count_of_rows
    moment = slab_first + jnp.arange(count_of_rows)
    back_time = moment - offsets[0]
    target = jnp.where(back_time >= 0, back_time, moment + offsets[0])
    local_index = target - slab_first + OFF_MAX
    matched_sample_vector = extended[local_index].astype(jnp.float32)
    own_first = lax.axis_index("batch") * count_of_rows
    piece_embed = lax.all_gather(embed, "batch", axis=0, tiled=True)
    portion_valid = lax.all_gather(live_flags, "batch", axis=0, tiled=True)
    couple_coefficient = pair_weights(
        embed, piece_embed, portion_valid.astype(jnp.float32), own_first
    )
    denom = jnp.sum(couple_coefficient, axis=1)
    piece_embed = lax.all_gather(embed.astype(jnp.float32), "batch", axis=0, tiled=True)
    portion_valid = lax.all_gather(usable_mask_vector, "batch", axis=0, tiled=True)
    piece_denom = lax.all_gather(denom, "batch", axis=0, tiled=True)
    add_piece_embed = piece_embed.astype(jnp.bfloat16)
    couple_coefficient = pair_weights(embed, add_piece_embed, portion_valid, own_first)
    soft = (couple_coefficient / denom[:, None]).astype(jnp.bfloat16)
    reverse = (couple_coefficient * usable_mask_vector[:, None] / piece_denom[None, :]).astype(
        jnp.bfloat16
    )
    anchor_sum = jnp.dot(soft, add_piece_embed, preferred_element_type=jnp.float32)
    pooled_sum = jnp.dot(reverse, add_piece_embed, preferred_element_type=jnp.float32)
    anchor_sum, pooled_sum = (anchor_sum, pooled_sum)
    propagated_samples = (
        jnp.zeros((OFF_MAX + count_of_rows, embed.shape[1]), jnp.float32)
        .at[local_index]
        .add(usable_mask_vector[:, None] * embed.astype(jnp.float32))
    )
    returned = passed_along(propagated_samples[:OFF_MAX], "tm", -1)
    pushed_own = propagated_samples[OFF_MAX:].at[count_of_rows - OFF_MAX :].add(returned)
    unit_length_derivative = reciprocal_softness * (
        usable_mask_vector[:, None] * (anchor_sum - matched_sample_vector) + pooled_sum - pushed_own
    )
    along = jnp.sum(unit * unit_length_derivative, axis=1, keepdims=True)
    grad_feat = ((unit_length_derivative - unit * along) * scale[:, None]).astype(jnp.bfloat16)
    grad_proj = lax.dot_general(
        hidden_two, grad_feat, (((0,), (0,)), ((), ())), preferred_element_type=jnp.float32
    )
    grad_hidden = lax.dot_general(
        grad_feat, proj_weight, (((1,), (1,)), ((), ())), preferred_element_type=jnp.float32
    )
    unused, pull = jax.vjp(jax.nn.gelu, second_preactivation)
    gradient_preactivation = pull(grad_hidden)[0].astype(jnp.bfloat16)
    grad_bias = jnp.sum(gradient_preactivation.astype(jnp.float32), axis=0)
    grad_conv = jnp.stack(
        [
            lax.dot_general(
                first_padded[
                    filter_tap_index * SECOND_DILATION : filter_tap_index * SECOND_DILATION
                    + count_of_rows
                ],
                gradient_preactivation,
                (((0,), (0,)), ((), ())),
                preferred_element_type=jnp.float32,
            )
            for filter_tap_index in range(3)
        ]
    )
    share = channels // slab_count
    conv_total, bias_total, proj_total = lax.psum(
        (grad_conv, grad_bias, grad_proj), ("tm", "batch", "rep")
    )
    conv_part = lax.dynamic_slice_in_dim(conv_total, slab_index * share, share, 2)
    bias_part = lax.dynamic_slice_in_dim(bias_total, slab_index * share, share, 0)
    proj_part = lax.dynamic_slice_in_dim(proj_total, slab_index * share, share, 0)
    return (embed[None], conv_part, bias_part, proj_part)


def solution(mesh):
    return jax.shard_map(
        per_device,
        mesh=mesh,
        in_specs=(
            P(("groups", "batch", "rep"), "tm", None),
            P(("groups", "batch", "rep")),
            P(),
            P(),
            P(),
            P(),
            P(),
            P(),
            P(),
            P(("groups", "batch", "rep"), "tm"),
            P(("groups", "batch", "rep"), "tm"),
        ),
        out_specs=(
            P(("groups", "batch", "rep"), "tm", None),
            P("groups", None, "tm"),
            P(("groups", "tm")),
            P(("groups", "tm"), None),
        ),
        check_vma=False,
    )
```

profile of v0, /device:TPU:0, one launch (start us, length us, event | category | flops | bytes accessed | tf_op | source)
XLA Modules:
  0.0 196.3 jit_solution(15781710611473754294)
XLA Ops:
  9.7 1.2 fusion.6
  10.9 1.3 collective-permute-start.1
  12.2 5.6 %collective-permute-start = (bf16[1,512]{1,0:T(2,128)(2,1)S(1)}, bf16[1,512]{1,0:T(2,128)(2,1)S(1)}, u32[]{:S(2)}, u32[]{:S(2)}) collective-permute-start(bf16[1,512]{1,0:T(2,128)(2,1)S(1)} %get-tuple-element.21), channel_id=1, source_target_pairs={{0,4},{4,8},{8,12},{1,5},{5,9},{9,13},{2,6},{6,10},{10,14},{3,7},{... | collective-permute-start | bytes 3080 | tf_op jit(solution)/shard_map/ppermute | solution.py:19
  18.5 4.3 %all-gather.1 = bf16[2,1,512]{2,1,0:T(2,128)(2,1)S(1)} all-gather(bf16[1,1,512]{2,1,0:T(2,128)(2,1)S(1)} %reshape.147), channel_id=1, replica_groups=mesh['groups'=2,'tm'=4,'batch'=2,'rep'=2] {'batch'}, dimensions={0}, use_global_device_ids=true | all-gather | bytes 3072 | tf_op jit(solution)/shard_map/all_gather | solution.py:112
  23.5 1.6 fusion.27
  25.2 4.3 %all-gather = f32[2,1,512]{2,1,0:T(1,128)S(1)} all-gather(f32[1,1,512]{2,1,0:T(1,128)S(1)} %bitcast.87), channel_id=1, replica_groups=mesh['groups'=2,'tm'=4,'batch'=2,'rep'=2] {'batch'}, dimensions={0}, use_global_device_ids=true | all-gather | bytes 6144 | tf_op jit(solution)/shard_map/all_gather | solution.py:118
  30.8 1.3 collective-permute-start.3
  32.1 4.5 %collective-permute-start.2 = (bf16[2,512]{1,0:T(2,128)(2,1)S(1)}, bf16[2,512]{1,0:T(2,128)(2,1)S(1)}, u32[]{:S(2)}, u32[]{:S(2)}) collective-permute-start(bf16[2,512]{1,0:T(2,128)(2,1)S(1)} %get-tuple-element.19), channel_id=1, source_target_pairs={{0,4},{4,8},{8,12},{1,5},{5,9},{9,13},{2,6},{6,10},{10,14},{3,7},{... | collective-permute-start | bytes 6152 | tf_op jit(solution)/shard_map/ppermute | solution.py:19
  38.4 1.7 add_convert_fusion
  40.7 6.7 %all_gather.15 = bf16[1024,128]{1,0:T(8,128)(2,1)S(1)} all-gather(bf16[512,128]{1,0:T(8,128)(2,1)S(1)} %multiply_convert_fusion.1), channel_id=1, replica_groups=mesh['groups'=2,'tm'=4,'batch'=2,'rep'=2] {'batch'}, dimensions={0}, use_global_device_ids=true | all-gather | bytes 393216 | tf_op jit(solution)/shard_map/all_gather | solution.py:117
  47.4 5.6 %all_gather.17 = bf16[1024,128]{1,0:T(8,128)(2,1)S(1)} all-gather(bf16[512,128]{1,0:T(8,128)(2,1)S(1)} %multiply_convert_fusion.1), channel_id=1, replica_groups=mesh['groups'=2,'tm'=4,'batch'=2,'rep'=2] {'batch'}, dimensions={0}, use_global_device_ids=true | all-gather | bytes 393216 | tf_op jit(solution)/shard_map/all_gather | solution.py:111
  53.0 3.9 %collective-permute-start.4 = (bf16[10,128]{1,0:T(8,128)(2,1)S(1)}, bf16[10,128]{1,0:T(8,128)(2,1)S(1)}, u32[]{:S(2)}, u32[]{:S(2)}) collective-permute-start(bf16[10,128]{1,0:T(8,128)(2,1)S(1)} %slice.101), channel_id=1, source_target_pairs={{0,4},{4,8},{8,12},{1,5},{5,9},{9,13},{2,6},{6,10},{10,14},{3,7},{... | collective-permute-start | bytes 7688 | tf_op jit(solution)/shard_map/ppermute | solution.py:30
  56.9 2.5 %scatter_custom_fusion = f32[522,128]{1,0:T(8,128)S(1)} fusion(s32[512]{0:T(512)S(1)} %bitcast.93, f32[]{:T(128)} %constant.57.clone.1, f32[512]{0:T(512)S(1)} %fusion.52, f32[512,128]{1,0:T(8,128)S(1)} %get-tuple-element.25, f32[512]{0:T(512)S(1)} %add_rsqrt_fusion), kind=kCustom, calls=%fused_computation.74 | custom fusion | flops 327680 | bytes 533508 | tf_op jit(solution)/shard_map/scatter-add | solution.py:132
  59.4 1.3 collective-permute-start.5
  63.6 4.3 %all-gather.2 = f32[2,1,512]{2,1,0:T(1,128)S(1)} all-gather(f32[1,1,512]{2,1,0:T(1,128)S(1)} %bitcast.97), channel_id=1, replica_groups=mesh['groups'=2,'tm'=4,'batch'=2,'rep'=2] {'batch'}, dimensions={0}, use_global_device_ids=true | all-gather | bytes 6144 | tf_op jit(solution)/shard_map/all_gather | solution.py:119
  68.0 1.3 gather_fusion
  69.6 2.3 %multiply_reduce_fusion.1 = (f32[512]{0:T(512)S(1)}, f32[512,128]{1,0:T(8,128)S(1)}) fusion(f32[512,128]{1,0:T(8,128)S(1)} %get-tuple-element.25, f32[512]{0:T(512)S(1)} %add_rsqrt_fusion, f32[512,128]{1,0:T(8,128)S(1)} %scatter-add.13, bf16[1024,128]{1,0:T(8,128)(2,1)S(1)} %all_gather.15, f32[512,1024]{1,0:T(8,128)} %copy-done.6, f32[1024]{0:T(1024)S(1)} %bitcast.95, ...), kind=kOutput, calls=%fused_computation.73 | convolution fusion | flops 136379904 | bytes 3549184 | tf_op jit(solution)/shard_map/dot_general | solution.py:127
  72.1 1.0 fusion.75
  73.1 0.9 convert_reduce_fusion
  75.4 2.0 %pad_maximum_fusion = f32[3,512,512]{2,1,0:T(8,128)} fusion(f32[1,512,512]{2,1,0:T(8,128)S(1)} %convolution_bitcast_fusion, f32[1,512,512]{2,1,0:T(8,128)S(1)} %convolution_bitcast_fusion.1, f32[1,512,512]{2,1,0:T(8,128)S(1)} %convolution_bitcast_fusion.2), kind=kLoop, calls=%fused_computation.2 | loop fusion | flops 1572864 | bytes 6291456 | tf_op jit(solution)/shard_map/stack | solution.py:150
  78.2 31.2 %psum.22 = f32[512]{0:T(512)S(1)} all-reduce(f32[512]{0:T(512)S(1)} %get-tuple-element.28), channel_id=1, replica_groups=mesh['groups'=2,'tm'=4,'batch'=2,'rep'=2] {'tm','batch','rep'}, use_global_device_ids=true, to_apply=%region_6.7 | all-reduce | flops 512 | bytes 4096 | tf_op jit(solution)/shard_map/psum | solution.py:165
  110.0 75.9 %all-reduce.3.cloned.1.call-done = (f32[3,512,512]{2,1,0:T(8,128)}, f32[512,128]{1,0:T(8,128)}) async-done(((f32[3,512,512]{2,1,0:T(8,128)}, f32[512,128]{1,0:T(8,128)}), (f32[3,512,512]{2,1,0:T(8,128)}, f32[512,128]{1,0:T(8,128)})) %all-reduce.3.cloned.1.call-update) | async-done | bytes 3407888 | tf_op jit(solution)/shard_map/psum | solution.py:165
  185.9 2.1 %constant_dynamic-slice_fusion.1 = f32[3,512,128]{2,1,0:T(8,128)} fusion(f32[3,512,512]{2,1,0:T(8,128)} %get-tuple-element.16, s32[]{:T(128)S(6)} %select_n.38), kind=kLoop, calls=%fused_computation.103 | loop fusion | bytes 1572868 | tf_op jit(solution)/shard_map/dynamic_slice | solution.py:168
  188.0 1.5 constant_dynamic-slice_fusion
  (55 shorter events, 12.1 us)
Async XLA Ops:
  7.2 33.0 %copy-start = (bf16[512,128]{1,0:T(8,128)(2,1)S(1)}, bf16[512,128]{1,0:T(8,128)(2,1)}, u32[]{:S(2)}) copy-start(bf16[512,128]{1,0:T(8,128)(2,1)} %param.21) | copy-start | bytes 393220
  7.2 22.3 %copy-start.2 = (bf16[3,512,512]{2,1,0:T(8,128)(2,1)S(1)}, bf16[3,512,512]{2,1,0:T(8,128)(2,1)}, u32[]{:S(2)}) copy-start(bf16[3,512,512]{2,1,0:T(8,128)(2,1)} %param.17) | copy-start | bytes 4718596
  7.2 22.3 %copy-start.3 = (f32[512]{0:T(512)S(1)}, f32[512]{0:T(512)}, u32[]{:S(2)}) copy-start(f32[512]{0:T(512)} %param.18) | copy-start | bytes 6148
  7.2 178.7 %all-reduce.3.cloned.1.call-start = ((), (), s32[]{:S(2)}) async-start(), calls=%async_computation | async-start | bytes 6815744 | tf_op jit(solution)/shard_map/psum | solution.py:165
  10.9 19.1 %collective-permute-start.1 = (bf16[1,512]{1,0:T(2,128)(2,1)S(1)}, bf16[1,512]{1,0:T(2,128)(2,1)S(1)}, u32[]{:S(2)}, u32[]{:S(2)}) collective-permute-start(bf16[1,512]{1,0:T(2,128)(2,1)S(1)} %get-tuple-element.20), channel_id=1, source_target_pairs={{4,0},{8,4},{12,8},{5,1},{9,5},{13,9},{6,2},{10,6},{14,10},{7,3},{... | collective-permute-start | bytes 3080 | tf_op jit(solution)/shard_map/ppermute | solution.py:22
  12.2 17.3 %collective-permute-start = (bf16[1,512]{1,0:T(2,128)(2,1)S(1)}, bf16[1,512]{1,0:T(2,128)(2,1)S(1)}, u32[]{:S(2)}, u32[]{:S(2)}) collective-permute-start(bf16[1,512]{1,0:T(2,128)(2,1)S(1)} %get-tuple-element.21), channel_id=1, source_target_pairs={{0,4},{4,8},{8,12},{1,5},{5,9},{9,13},{2,6},{6,10},{10,14},{3,7},{... | collective-permute-start | bytes 3080 | tf_op jit(solution)/shard_map/ppermute | solution.py:19
  30.0 6.7 %copy-start.1 = (bf16[3,512,512]{2,1,0:T(8,128)(2,1)S(1)}, bf16[3,512,512]{2,1,0:T(8,128)(2,1)}, u32[]{:S(2)}) copy-start(bf16[3,512,512]{2,1,0:T(8,128)(2,1)} %param.19) | copy-start | bytes 4718596
  30.8 7.2 %copy-start.4 = (f32[512]{0:T(512)S(1)}, f32[512]{0:T(512)}, u32[]{:S(2)}) copy-start(f32[512]{0:T(512)} %param.20) | copy-start | bytes 6148
  30.8 7.6 %collective-permute-start.3 = (bf16[2,512]{1,0:T(2,128)(2,1)S(1)}, bf16[2,512]{1,0:T(2,128)(2,1)S(1)}, u32[]{:S(2)}, u32[]{:S(2)}) collective-permute-start(bf16[2,512]{1,0:T(2,128)(2,1)S(1)} %get-tuple-element.18), channel_id=1, source_target_pairs={{4,0},{8,4},{12,8},{5,1},{9,5},{13,9},{6,2},{10,6},{14,10},{7,3},{... | collective-permute-start | bytes 6152 | tf_op jit(solution)/shard_map/ppermute | solution.py:22
  32.1 5.8 %collective-permute-start.2 = (bf16[2,512]{1,0:T(2,128)(2,1)S(1)}, bf16[2,512]{1,0:T(2,128)(2,1)S(1)}, u32[]{:S(2)}, u32[]{:S(2)}) collective-permute-start(bf16[2,512]{1,0:T(2,128)(2,1)S(1)} %get-tuple-element.19), channel_id=1, source_target_pairs={{0,4},{4,8},{8,12},{1,5},{5,9},{9,13},{2,6},{6,10},{10,14},{3,7},{... | collective-permute-start | bytes 6152 | tf_op jit(solution)/shard_map/ppermute | solution.py:19
  53.0 15.0 %collective-permute-start.4 = (bf16[10,128]{1,0:T(8,128)(2,1)S(1)}, bf16[10,128]{1,0:T(8,128)(2,1)S(1)}, u32[]{:S(2)}, u32[]{:S(2)}) collective-permute-start(bf16[10,128]{1,0:T(8,128)(2,1)S(1)} %slice.101), channel_id=1, source_target_pairs={{0,4},{4,8},{8,12},{1,5},{5,9},{9,13},{2,6},{6,10},{10,14},{3,7},{... | collective-permute-start | bytes 7688 | tf_op jit(solution)/shard_map/ppermute | solution.py:30
  59.4 10.0 %collective-permute-start.5 = (f32[10,128]{1,0:T(8,128)S(1)}, f32[10,128]{1,0:T(8,128)S(1)}, u32[]{:S(2)}, u32[]{:S(2)}) collective-permute-start(f32[10,128]{1,0:T(8,128)S(1)} %slice.104), channel_id=1, source_target_pairs={{4,0},{8,4},{12,8},{5,1},{9,5},{13,9},{6,2},{10,6},{14,10},{7,3},{... | collective-permute-start | bytes 15368 | tf_op jit(solution)/shard_map/ppermute | solution.py:30
  62.3 1.3 copy-start.6
  69.5 3.6 %copy-start.5 = (f32[512,512]{1,0:T(8,128)S(1)}, f32[512,512]{1,0:T(8,128)}, u32[]{:S(2)}) copy-start(f32[512,512]{1,0:T(8,128)} %get-tuple-element.23) | copy-start | bytes 3145732
Sparse Core Ops, SparseCore 0:
  77.5 108.3 all-reduce.2
where the time goes:
time: 197 us; the launch traced here: 196 us
  waiting for transfers between devices  76.8 us (39%)
  blocking collectives  56.5 us (29%)
  starting transfers between devices  17.9 us (9%)
  between operations  15.8 us (8%)
  matrix products  15.2 us (8%)
  other arithmetic  7.54 us (4%)
  local copies, waits for them, and re-layouts  6.55 us (3%)
    psum x1, waiting for transfers between devices, per_device(): lax.psum((grad_conv, grad_bias, grad_proj), ('tm', 'batch', 'rep'))  75.9 us
    psum x1, blocking collectives, per_device(): lax.psum((grad_conv, grad_bias, grad_proj), ('tm', 'batch', 'rep'))  31.2 us
    ppermute x2, starting transfers between devices, padded_2(): lax.ppermute(lax.slice_in_dim(block, block.shape[dim] - width, None, axis...  10.1 us
    all_gather x1, blocking collectives, per_device(): lax.all_gather(embed.astype(jnp.float32), 'batch', axis=0, tiled=True)  6.66 us
    all_gather x1, blocking collectives, per_device(): piece_embed = lax.all_gather(embed, 'batch', axis=0, tiled=True)  5.63 us
    dot_general x6, matrix products, convolved_rows(): jnp.dot(shifted, couple_coefficient[filter_tap_index], preferred_element_...  5.48 us
    ppermute x2, starting transfers between devices, passed_along(): lax.ppermute(value, axis, [(source, source + steps) for source in range(l...  5.17 us
    all_gather x1, blocking collectives, per_device(): portion_valid = lax.all_gather(live_flags, 'batch', axis=0, tiled=True)  4.34 us
  transfers between devices with their start and end apart: 7, of which 2 were waited for; matrix products, arithmetic and copies ran while one was open for 6% of the time, Pallas kernels for 0%

commit v1 on v0

v1 whole, which is shorter than its diff:
```python
import functools

import jax
import jax.numpy as jnp
from jax import lax
from jax.experimental import pallas as pl
from jax.experimental.pallas import tpu as pltpu
from jax.sharding import PartitionSpec as P

OFF_MAX = 10
HALO = 16
PAD = 8
LANES = 128
F32 = jnp.float32
BF16 = jnp.bfloat16
GELU_C = 0.7978845608028654
GELU_A = 0.044715


def gelu_parts(x):
    square = x * x
    th = jnp.tanh(GELU_C * x * (1.0 + GELU_A * square))
    half = 0.5 * (1.0 + th)
    slope = half + (0.5 * GELU_C) * x * (1.0 - th * th) * (1.0 + (3.0 * GELU_A) * square)
    return x * half, slope


def kernel(
    n_tm, n_batch, chunks,
    ids_ref, counts_ref, lat_ref, gain_ref, shift_ref, w1_hbm, b1_ref, w2_hbm, b2_ref, proj_ref, off_ref,
    emb_out, conv_out, bias_out, proj_out,
    w1, w2, wsem, halo, meta, meta_next, meta_pool, ext, taps, pre, slope, hid2, unit_s, scale_s, emb_ext, pool,
    xs, rhs, gt, grads, rep_in, part_one, batch_in, part_two, tm_in, final, tmp,
    halo_sem, meta_sem, mpool_sem, pool_sem, rep_sem, batch_sem, tm_sem, gat_sem, fin_sem,
):
    rows, channels = lat_ref.shape
    total = rows + 2 * HALO
    share = channels // n_tm
    piece = share // n_batch
    z = lax.axis_index("tm")
    b = lax.axis_index("batch")
    r = lax.axis_index("rep")
    other = 1 - r
    load1 = pltpu.make_async_copy(w1_hbm, w1, wsem.at[0])
    load2 = pltpu.make_async_copy(w2_hbm, w2, wsem.at[1])
    load1.start()
    load2.start()
    meta[0:1, :] = off_ref[0:1, 0:LANES]
    meta[1:2, :] = jnp.full((1, LANES), counts_ref[0, 0], jnp.int32)
    meta[2:8, :] = jnp.zeros((6, LANES), jnp.int32)

    barrier = pltpu.get_barrier_semaphore()

    def tm_at(o):
        return {"tm": lax.rem(z + o, n_tm)}

    def batch_at(o):
        return {"batch": lax.rem(b + o, n_batch)}

    peers = [tm_at(o) for o in range(1, n_tm)] + [batch_at(o) for o in range(1, n_batch)] + [{"rep": other}]
    for peer in peers:
        pl.semaphore_signal(barrier, inc=1, device_id=peer, device_id_type=pl.DeviceIdType.MESH)
    pl.semaphore_wait(barrier, len(peers))

    started = []

    def send(src, dst, sems, index, peer):
        copy = pltpu.make_async_remote_copy(
            src_ref=src, dst_ref=dst, send_sem=sems.at[(0,) + index], recv_sem=sems.at[(1,) + index],
            device_id=peer, device_id_type=pl.DeviceIdType.MESH,
        )
        copy.start()
        started.append(copy)
        return copy

    low = send(lat_ref.at[pl.ds(rows - HALO, HALO)], halo.at[0], halo_sem, (0,), tm_at(1))
    high = send(lat_ref.at[pl.ds(0, HALO)], halo.at[1], halo_sem, (1,), tm_at(n_tm - 1))
    nextm = send(meta, meta_next, meta_sem, (0,), tm_at(n_tm - 1))
    mpools = [send(meta, meta_pool.at[o - 1], mpool_sem, (o - 1,), batch_at(o)) for o in range(1, n_batch)]

    pick = lax.broadcasted_iota(jnp.int32, gain_ref.shape, 0) == ids_ref[0]
    gain = jnp.sum(jnp.where(pick, gain_ref[...], 0.0), axis=0, keepdims=True)
    shift = jnp.sum(jnp.where(pick, shift_ref[...], 0.0), axis=0, keepdims=True)

    def based(block):
        return (block.astype(F32) * gain + shift).astype(BF16).astype(F32)

    ext[0:PAD, :] = jnp.zeros((PAD, channels), F32)
    ext[PAD + total :, :] = jnp.zeros((PAD, channels), F32)
    ext[PAD + HALO : PAD + HALO + rows, :] = based(lat_ref[...])
    low.wait_recv()
    high.wait_recv()
    has_low = z > 0
    has_high = z < n_tm - 1
    ext[PAD : PAD + HALO, :] = jnp.where(has_low, based(halo[0]), 0.0)
    ext[PAD + HALO + rows : PAD + total, :] = jnp.where(has_high, based(halo[1]), 0.0)

    half = total // 2
    starts = (0, half)

    def gather_taps(dilation):
        for k in range(3):
            first = PAD + (k - 1) * dilation
            taps[:, k * channels : (k + 1) * channels] = ext[first : first + total, :].astype(BF16)

    gather_taps(1)
    load1.wait()
    for s in starts:
        pre[s : s + half, :] = jnp.dot(taps[s : s + half, :], w1[...], preferred_element_type=F32)
    for s in starts:
        x = pre[s : s + half, :] + b1_ref[...]
        value = 0.5 * x * (1.0 + jnp.tanh(GELU_C * x * (1.0 + GELU_A * x * x)))
        hid = (ext[PAD + s : PAD + s + half, :] + value).astype(BF16).astype(F32)
        at = s + lax.broadcasted_iota(jnp.int32, (half, 1), 0)
        inside = jnp.logical_and(
            jnp.logical_or(has_low, at >= HALO), jnp.logical_or(has_high, at < HALO + rows)
        )
        ext[PAD + s : PAD + s + half, :] = jnp.where(inside, hid, 0.0)
    gather_taps(2)
    load2.wait()
    for s in starts:
        pre[s : s + half, :] = jnp.dot(taps[s : s + half, :], w2[...], preferred_element_type=F32)
    for s in starts:
        value, deriv = gelu_parts(pre[s : s + half, :] + b2_ref[...])
        slope[s : s + half, :] = deriv
        hid = (ext[PAD + s : PAD + s + half, :] + value).astype(BF16)
        hid2[s : s + half, :] = hid
        feats = jnp.dot(hid, proj_ref[...], preferred_element_type=F32)
        scale = lax.rsqrt(jnp.sum(feats * feats, axis=1, keepdims=True) + 1e-06)
        unit = feats * scale
        unit_s[s : s + half, :] = unit
        scale_s[s : s + half, :] = jnp.broadcast_to(scale, (half, LANES))
        emb_ext[s : s + half, :] = unit.astype(BF16)
    own = emb_ext[HALO : HALO + rows, :]
    emb_out[...] = own
    pool[0] = own
    pools = [send(pool.at[0], pool.at[o], pool_sem, (o - 1,), batch_at(o)) for o in range(1, n_batch)]

    own_count = meta[1:2, 0:1]
    col = lax.broadcasted_iota(jnp.int32, (rows, 1), 0)
    row = lax.broadcasted_iota(jnp.int32, (1, rows), 1)
    live = (col < own_count).astype(F32)
    first = z * rows
    offs_row = off_ref[...]
    offs_col = jnp.transpose(jnp.broadcast_to(offs_row.astype(F32), (LANES, rows)))[:, 0:1].astype(jnp.int32)
    target_col = jnp.where(first + col - offs_col >= 0, col - offs_col, col + offs_col)
    target_row = jnp.where(first + row - offs_row >= 0, row - offs_row, row + offs_row)
    live_row = (row < own_count).astype(F32)
    band = jnp.where(target_col == row, live, 0.0) + jnp.where(target_row == col, live_row, 0.0)
    paired = jnp.dot(band.astype(BF16), own, preferred_element_type=F32)
    edge = lax.broadcasted_iota(jnp.int32, (1, HALO), 1)
    band_low = jnp.where(target_col == edge - HALO, live, 0.0)
    paired += jnp.dot(band_low.astype(BF16), emb_ext[0:HALO, :], preferred_element_type=F32)
    nextm.wait_recv()
    next_off = meta_next[0:1, 0:HALO]
    next_live = jnp.where(jnp.logical_and(has_high, edge < meta_next[1:2, 0:HALO]), 1.0, 0.0)
    band_high = jnp.where(rows + edge - next_off == col, next_live, 0.0)
    paired += jnp.dot(band_high.astype(BF16), emb_ext[HALO + rows :, :], preferred_element_type=F32)

    for copy in mpools:
        copy.wait_recv()

    def count_of(m):
        return own_count if m == 0 else meta_pool[m - 1, 1:2, 0:1]

    diag = col == row

    def scored(a_block, m):
        s = lax.dot_general(a_block, pool[m], (((1,), (1,)), ((), ())), preferred_element_type=F32)
        return jnp.exp(2.0 * s - 2.0)

    def summed(x, m):
        return jnp.sum(jnp.where(row < count_of(m), x, 0.0), axis=1, keepdims=True)

    x0 = jnp.where(diag, 0.0, scored(own, 0))
    xs[0] = x0.astype(BF16)
    denom = summed(x0, 0)
    for copy in pools:
        copy.wait_recv()
    for m in range(1, n_batch):
        x = scored(own, m)
        xs[m] = x.astype(BF16)
        denom += summed(x, m)

    def set_rhs(a, a_live, a_denom):
        block = pool[a].astype(F32) * a_live
        rhs[a, :, 0:LANES] = block.astype(BF16)
        rhs[a, :, LANES : 2 * LANES] = (block / a_denom).astype(BF16)

    set_rhs(0, live, denom)
    if n_batch == 2:
        other_denom = summed(scored(pool[1], 0), 0)
        other_denom += summed(jnp.where(diag, 0.0, scored(pool[1], 1)), 1)
        set_rhs(1, (col < count_of(1)).astype(F32), other_denom)
    else:
        def one(a, carry):
            block = pool[a]
            den = jnp.zeros((rows, 1), F32)
            for m in range(n_batch):
                den += summed(jnp.where(jnp.logical_and(diag, a == m), 0.0, scored(block, m)), m)
            a_count = meta_pool[a - 1][1:2, 0:1]
            set_rhs(a, (col < a_count).astype(F32), den)
            return carry

        lax.fori_loop(1, n_batch, one, 0)
    acc = jnp.dot(xs[0], rhs[0], preferred_element_type=F32)
    for m in range(1, n_batch):
        acc += jnp.dot(xs[m], rhs[m], preferred_element_type=F32)
    unit = unit_s[HALO : HALO + rows, :]
    scale = scale_s[HALO : HALO + rows, :]
    grad_unit = 2.0 * (live * (acc[:, 0:LANES] / denom + acc[:, LANES:]) - paired)
    along = jnp.sum(unit * grad_unit, axis=1, keepdims=True)
    gf = ((grad_unit - unit * along) * scale).astype(BF16)
    gh = lax.dot_general(gf, proj_ref[...], (((1,), (1,)), ((), ())), preferred_element_type=F32)
    gp = (gh * slope[HALO : HALO + rows, :]).astype(BF16)
    gt[...] = jnp.transpose(gp)

    def put(owner, c, value):
        if piece % 16 == 0:
            grads[owner, c] = jnp.swapaxes(
                value.astype(BF16).reshape(n_tm, n_batch, piece, LANES), 0, 1
            )
        else:
            tmp[...] = value
            for i in range(n_tm):
                for j in range(n_batch):
                    at = i * share + j * piece
                    grads[owner, c, j, i] = tmp[at : at + piece, :].astype(BF16)

    reps = []
    for c in range(chunks):
        if c < chunks - 1:
            value = jnp.dot(
                gt[...], taps[HALO : HALO + rows, 2 * c * LANES : 2 * (c + 1) * LANES], preferred_element_type=F32
            )
            put(0, c, value[:, 0:LANES])
            put(1, c, value[:, LANES:])
        else:
            put(0, c, lax.dot_general(
                hid2[HALO : HALO + rows, :], gf, (((0,), (0,)), ((), ())), preferred_element_type=F32
            ))
            put(1, c, jnp.dot(gt[...], jnp.ones((rows, LANES), BF16), preferred_element_type=F32))
        reps.append(send(grads.at[other, c], rep_in.at[c], rep_sem, (c,), {"rep": other}))

    bats = []
    for c in range(chunks):
        reps[c].wait_recv()
        part_one[c] = (grads[r, c].astype(F32) + rep_in[c].astype(F32)).astype(BF16)
        bats.append([
            send(part_one.at[c, lax.rem(b + o, n_batch)], batch_in.at[c, o - 1], batch_sem, (c, o - 1), batch_at(o))
            for o in range(1, n_batch)
        ])
    tms = []
    for c in range(chunks):
        value = part_one[c, b].astype(F32)
        for o in range(1, n_batch):
            bats[c][o - 1].wait_recv()
            value += batch_in[c, o - 1].astype(F32)
        part_two[c] = value.astype(BF16)
        tms.append([
            send(part_two.at[c, lax.rem(z + o, n_tm)], tm_in.at[c, o - 1], tm_sem, (c, o - 1), tm_at(o))
            for o in range(1, n_tm)
        ])
    gats = []
    for c in range(chunks):
        value = part_two[c, z].astype(F32)
        for o in range(1, n_tm):
            tms[c][o - 1].wait_recv()
            value += tm_in[c, o - 1].astype(F32)
        final[r, c, b] = value.astype(BF16)
        gats.append([
            send(final.at[r, c, b], final.at[r, c, b], gat_sem, (c, o - 1), batch_at(o)) for o in range(1, n_batch)
        ])
    fins = []
    for c in range(chunks):
        for copy in gats[c]:
            copy.wait_recv()
        fins.append(send(final.at[r, c], final.at[r, c], fin_sem, (c,), {"rep": other}))
    per_tap = channels // LANES
    for c in range(chunks):
        fins[c].wait_recv()
        for owner in range(2):
            if piece % 16 == 0:
                value = final[owner, c].astype(F32).reshape(share, LANES)
            else:
                for j in range(n_batch):
                    tmp[j * piece : (j + 1) * piece, :] = final[owner, c, j].astype(F32)
                value = tmp[0:share, :]
            chunk = 2 * c + owner
            if c < chunks - 1:
                k, part = divmod(chunk, per_tap)
                conv_out[k, part * LANES : (part + 1) * LANES, :] = jnp.transpose(value)
            elif owner == 0:
                proj_out[...] = value
            else:
                bias_out[...] = jnp.transpose(value)[0:1, :]
    for copy in started:
        copy.wait_send()


def per_device(
    n_tm, n_batch,
    latents, session_ids, session_gain, session_shift, first_conv_weight, first_conv_bias,
    second_conv_weight, second_conv_bias, proj_weight, offsets, counts,
):
    rows, channels = latents.shape[1:]
    emb = proj_weight.shape[1]
    total = rows + 2 * HALO
    share = channels // n_tm
    piece = share // n_batch
    chunks = (3 * channels // LANES + 2) // 2
    vmem = pl.BlockSpec(memory_space=pltpu.VMEM)
    smem = pl.BlockSpec(memory_space=pltpu.SMEM)
    hbm = pl.BlockSpec(memory_space=pl.ANY)
    nb = n_batch - 1
    dma = pltpu.SemaphoreType.DMA
    embed, conv, bias, proj = pl.pallas_call(
        functools.partial(kernel, n_tm, n_batch, chunks),
        out_shape=(
            jax.ShapeDtypeStruct((rows, emb), BF16),
            jax.ShapeDtypeStruct((3, channels, share), F32),
            jax.ShapeDtypeStruct((1, share), F32),
            jax.ShapeDtypeStruct((share, emb), F32),
        ),
        in_specs=[smem, smem, vmem, vmem, vmem, hbm, vmem, hbm, vmem, vmem, vmem],
        out_specs=(vmem, vmem, vmem, vmem),
        scratch_shapes=[
            pltpu.VMEM((3 * channels, channels), BF16),
            pltpu.VMEM((3 * channels, channels), BF16),
            dma((2,)),
            pltpu.VMEM((2, HALO, channels), BF16),
            pltpu.VMEM((8, LANES), jnp.int32),
            pltpu.VMEM((8, LANES), jnp.int32),
            pltpu.VMEM((nb, 8, LANES), jnp.int32),
            pltpu.VMEM((total + 2 * PAD, channels), F32),
            pltpu.VMEM((total, 3 * channels), BF16),
            pltpu.VMEM((total, channels), F32),
            pltpu.VMEM((total, channels), F32),
            pltpu.VMEM((total, channels), BF16),
            pltpu.VMEM((total, emb), F32),
            pltpu.VMEM((total, LANES), F32),
            pltpu.VMEM((total, emb), BF16),
            pltpu.VMEM((n_batch, rows, emb), BF16),
            pltpu.VMEM((n_batch, rows, rows), BF16),
            pltpu.VMEM((n_batch, rows, 2 * emb), BF16),
            pltpu.VMEM((channels, rows), BF16),
            pltpu.VMEM((2, chunks, n_batch, n_tm, piece, LANES), BF16),
            pltpu.VMEM((chunks, n_batch, n_tm, piece, LANES), BF16),
            pltpu.VMEM((chunks, n_batch, n_tm, piece, LANES), BF16),
            pltpu.VMEM((chunks, nb, n_tm, piece, LANES), BF16),
            pltpu.VMEM((chunks, n_tm, piece, LANES), BF16),
            pltpu.VMEM((chunks, n_tm - 1, piece, LANES), BF16),
            pltpu.VMEM((2, chunks, n_batch, piece, LANES), BF16),
            pltpu.VMEM((channels, LANES), F32),
            dma((2, 2)),
            dma((2, 1)),
            dma((2, nb)),
            dma((2, nb)),
            dma((2, chunks)),
            dma((2, chunks, nb)),
            dma((2, chunks, n_tm - 1)),
            dma((2, chunks, nb)),
            dma((2, chunks)),
        ],
        compiler_params=pltpu.CompilerParams(
            collective_id=0, has_side_effects=True, vmem_limit_bytes=56 * 1024 * 1024
        ),
    )(
        session_ids, counts, latents[0], session_gain, session_shift,
        first_conv_weight.reshape(3 * channels, channels), first_conv_bias[None],
        second_conv_weight.reshape(3 * channels, channels), second_conv_bias[None],
        proj_weight, offsets,
    )
    return embed[None], conv, bias[0], proj


def solution(mesh):
    return jax.shard_map(
        functools.partial(per_device, mesh.shape["tm"], mesh.shape["batch"]),
        mesh=mesh,
        in_specs=(
            P(("groups", "batch", "rep"), "tm", None),
            P(("groups", "batch", "rep")),
            P(),
            P(),
            P(),
            P(),
            P(),
            P(),
            P(),
            P(("groups", "batch", "rep"), "tm"),
            P(("groups", "batch", "rep"), "tm"),
        ),
        out_specs=(
            P(("groups", "batch", "rep"), "tm", None),
            P("groups", None, "tm"),
            P(("groups", "tm")),
            P(("groups", "tm"), None),
        ),
        check_vma=False,
    )
```

time: 197 us -> 49.7 us (0.25)
  waiting for transfers between devices: 76.8 us -> 0 us
  blocking collectives: 56.5 us -> 0 us
  Pallas kernels: 0 us -> 42.7 us
  starting transfers between devices: 17.9 us -> 0 us
  matrix products: 15.2 us -> 0 us
  between operations: 15.8 us -> 1.95 us
  other arithmetic: 7.54 us -> 0 us
    psum x1 -> x0, waiting for transfers between devices: 75.9 us -> none  [per_device(): lax.psum((grad_conv, grad_bias, grad_proj), ('tm', 'batch', 'rep'))]
    pallas_call x0 -> x1, Pallas kernels: none -> 42.7 us  [per_device(): pl.pallas_call(functools.partial(kernel, n_tm, n_batch, chunks), out_shap...]
    psum x1 -> x0, blocking collectives: 31.2 us -> none  [per_device(): lax.psum((grad_conv, grad_bias, grad_proj), ('tm', 'batch', 'rep'))]
    all_gather x5 -> x0, blocking collectives: 25.3 us -> none  [the longest x1 6.66 us: per_device(): lax.all_gather(embed.astype(jnp.float32), 'batch', axis=0, tiled=True)]
    ppermute x6 -> x0, starting transfers between devices: 17.9 us -> none  [the longest x2 10.1 us: padded_2(): lax.ppermute(lax.slice_in_dim(block, block.shape[dim] - width, None, axis...]
    dot_general x18 -> x0, matrix products: 15.2 us -> none  [the longest x6 5.48 us: convolved_rows(): jnp.dot(shifted, couple_coefficient[filter_tap_index], preferred_element_...]
    dynamic_slice x3 -> x0, local copies, waits for them, and re-layouts: 4.12 us -> none  [the longest x1 2.06 us: per_device(): lax.dynamic_slice_in_dim(conv_total, slab_index * share, share, 2)]
    unnamed x15 -> x8, local copies, waits for them, and re-layouts: 0.88 us -> 4.81 us
  transfers between devices with their start and end apart: 7 -> 0, of which waited for: 2 -> 0; matrix products, arithmetic and copies ran while one was open for 6% -> 0% of each run, Pallas kernels for 0% -> 0%
where the time goes in v1:
time: 49.7 us; the launch traced here: 49.4 us
  Pallas kernels  42.7 us (86%)
  local copies, waits for them, and re-layouts  4.81 us (10%)
  between operations  1.95 us (4%)
    pallas_call x1, Pallas kernels, per_device(): pl.pallas_call(functools.partial(kernel, n_tm, n_batch, chunks), out_shap...  42.7 us
    unnamed x8, local copies, waits for them, and re-layouts  4.81 us

profile of v1, /device:TPU:0, one launch (start us, length us, event | category | flops | bytes accessed | tf_op | source)
XLA Modules:
  0.0 49.4 jit_solution(15335317603242383260)
XLA Ops:
  1.9 42.7 %shard_map.138 = (bf16[512,128]{1,0:T(8,128)(2,1)}, f32[3,512,128]{2,1,0:T(8,128)}, f32[1,128]{1,0:T(1,128)}, f32[128,128]{1,0:T(8,128)}) custom-call(s32[1]{0:T(128)S(6)} %copy.19.ids_ref, s32[1,1]{1,0:T(1,128)S(6)} %copy.20.counts_ref, bf16[512,512]{1,0:T(8,128)(2,1)} %bitcast.9, f32[8,512]{1,0:T(8,128)} %gain_ref.1, f32[8,512]{1,0:T(8,128)} %shift_ref.1, ...), custom_call_target="tpu_custom_call" | custom-call | tf_op jit(solution)/shard_map/pallas_call | solution.py:317
  44.6 0.0 copy-start.1
  44.6 0.0 copy-start
  44.6 1.6 %copy.21 = bf16[1,512,128]{2,1,0:T(8,128)(2,1)} copy(bf16[1,512,128]{2,1,0:T(8,128)(2,1)} %bitcast.10) | data formatting | bytes 262144
  46.2 2.1 %copy.22 = f32[3,512,128]{2,1,0:T(8,128)} copy(f32[3,512,128]{2,1,0:T(8,128)} %get-tuple-element.17) | data formatting | bytes 1572864
  48.3 0.0 copy-done.1
  48.3 0.5 %copy.23 = f32[128]{0:T(128)} copy(f32[128]{0:T(128)S(1)} %bitcast.13) | data formatting | bytes 1024
  48.8 0.0 copy-done
  48.8 0.6 %copy.24 = f32[128,128]{1,0:T(8,128)} copy(f32[128,128]{1,0:T(8,128)S(1)} %copy-done) | data formatting | bytes 131072
Async XLA Ops:
  44.6 3.7 %copy-start.1 = (f32[1,128]{1,0:T(1,128)S(1)}, f32[1,128]{1,0:T(1,128)}, u32[]{:S(2)}) copy-start(f32[1,128]{1,0:T(1,128)} %get-tuple-element.10) | copy-start | bytes 1540
  44.6 4.2 %copy-start = (f32[128,128]{1,0:T(8,128)S(1)}, f32[128,128]{1,0:T(8,128)}, u32[]{:S(2)}) copy-start(f32[128,128]{1,0:T(8,128)} %get-tuple-element.19) | copy-start | bytes 196612

commit v2 on v1

--- a/solution.py
+++ b/solution.py
@@ -28,7 +28,7 @@
 def kernel(
     n_tm, n_batch, chunks,
     ids_ref, counts_ref, lat_ref, gain_ref, shift_ref, w1_hbm, b1_ref, w2_hbm, b2_ref, proj_ref, off_ref,
-    emb_out, conv_out, bias_out, proj_out,
+    emb_out, sums_out,
     w1, w2, wsem, halo, meta, meta_next, meta_pool, ext, taps, pre, slope, hid2, unit_s, scale_s, emb_ext, pool,
     xs, rhs, gt, grads, rep_in, part_one, batch_in, part_two, tm_in, final, tmp,
     halo_sem, meta_sem, mpool_sem, pool_sem, rep_sem, batch_sem, tm_sem, gat_sem, fin_sem,
@@ -46,7 +46,7 @@
     load1.start()
     load2.start()
     meta[0:1, :] = off_ref[0:1, 0:LANES]
-    meta[1:2, :] = jnp.full((1, LANES), counts_ref[0, 0], jnp.int32)
+    meta[1:2, :] = jnp.broadcast_to(counts_ref[...], (1, LANES))
     meta[2:8, :] = jnp.zeros((6, LANES), jnp.int32)
 
     barrier = pltpu.get_barrier_semaphore()
@@ -78,7 +78,7 @@
     nextm = send(meta, meta_next, meta_sem, (0,), tm_at(n_tm - 1))
     mpools = [send(meta, meta_pool.at[o - 1], mpool_sem, (o - 1,), batch_at(o)) for o in range(1, n_batch)]
 
-    pick = lax.broadcasted_iota(jnp.int32, gain_ref.shape, 0) == ids_ref[0]
+    pick = lax.broadcasted_iota(jnp.int32, gain_ref.shape, 0) == ids_ref[...]
     gain = jnp.sum(jnp.where(pick, gain_ref[...], 0.0), axis=0, keepdims=True)
     shift = jnp.sum(jnp.where(pick, shift_ref[...], 0.0), axis=0, keepdims=True)
 
@@ -88,35 +88,49 @@
     ext[0:PAD, :] = jnp.zeros((PAD, channels), F32)
     ext[PAD + total :, :] = jnp.zeros((PAD, channels), F32)
     ext[PAD + HALO : PAD + HALO + rows, :] = based(lat_ref[...])
-    low.wait_recv()
-    high.wait_recv()
+    ext[PAD : PAD + HALO, :] = jnp.zeros((HALO, channels), F32)
+    ext[PAD + HALO + rows : PAD + total, :] = jnp.zeros((HALO, channels), F32)
     has_low = z > 0
     has_high = z < n_tm - 1
-    ext[PAD : PAD + HALO, :] = jnp.where(has_low, based(halo[0]), 0.0)
-    ext[PAD + HALO + rows : PAD + total, :] = jnp.where(has_high, based(halo[1]), 0.0)
-
     half = total // 2
     starts = (0, half)
-
-    def gather_taps(dilation):
+    edge_rows = 2 * HALO
+    middle = total - 2 * edge_rows
+
+    def gather_taps(dilation, begin, count):
         for k in range(3):
-            first = PAD + (k - 1) * dilation
-            taps[:, k * channels : (k + 1) * channels] = ext[first : first + total, :].astype(BF16)
-
-    gather_taps(1)
-    load1.wait()
-    for s in starts:
-        pre[s : s + half, :] = jnp.dot(taps[s : s + half, :], w1[...], preferred_element_type=F32)
-    for s in starts:
-        x = pre[s : s + half, :] + b1_ref[...]
+            first = PAD + begin + (k - 1) * dilation
+            taps[begin : begin + count, k * channels : (k + 1) * channels] = ext[first : first + count, :].astype(BF16)
+
+    def first_hidden(begin, count):
+        x = pre[begin : begin + count, :] + b1_ref[...]
         value = 0.5 * x * (1.0 + jnp.tanh(GELU_C * x * (1.0 + GELU_A * x * x)))
-        hid = (ext[PAD + s : PAD + s + half, :] + value).astype(BF16).astype(F32)
-        at = s + lax.broadcasted_iota(jnp.int32, (half, 1), 0)
+        hid = (ext[PAD + begin : PAD + begin + count, :] + value).astype(BF16).astype(F32)
+        at = begin + lax.broadcasted_iota(jnp.int32, (count, 1), 0)
         inside = jnp.logical_and(
             jnp.logical_or(has_low, at >= HALO), jnp.logical_or(has_high, at < HALO + rows)
         )
-        ext[PAD + s : PAD + s + half, :] = jnp.where(inside, hid, 0.0)
-    gather_taps(2)
+        return jnp.where(inside, hid, 0.0)
+
+    gather_taps(1, edge_rows, middle)
+    load1.wait()
+    pre[edge_rows : edge_rows + middle, :] = jnp.dot(
+        taps[edge_rows : edge_rows + middle, :], w1[...], preferred_element_type=F32
+    )
+    low.wait_recv()
+    high.wait_recv()
+    ext[PAD : PAD + HALO, :] = jnp.where(has_low, based(halo[0]), 0.0)
+    ext[PAD + HALO + rows : PAD + total, :] = jnp.where(has_high, based(halo[1]), 0.0)
+    last = total - edge_rows
+    gather_taps(1, 0, edge_rows)
+    gather_taps(1, last, edge_rows)
+    ends = jnp.concatenate([taps[0:edge_rows, :], taps[last:, :]], axis=0)
+    ends = jnp.dot(ends, w1[...], preferred_element_type=F32)
+    pre[0:edge_rows, :] = ends[0:edge_rows, :]
+    pre[last:, :] = ends[edge_rows:, :]
+    for s in starts:
+        ext[PAD + s : PAD + s + half, :] = first_hidden(s, half)
+    gather_taps(2, 0, total)
     load2.wait()
     for s in starts:
         pre[s : s + half, :] = jnp.dot(taps[s : s + half, :], w2[...], preferred_element_type=F32)
@@ -227,8 +241,9 @@
                     at = i * share + j * piece
                     grads[owner, c, j, i] = tmp[at : at + piece, :].astype(BF16)
 
-    reps = []
-    for c in range(chunks):
+    reps = {}
+
+    def produce(c):
         if c < chunks - 1:
             value = jnp.dot(
                 gt[...], taps[HALO : HALO + rows, 2 * c * LANES : 2 * (c + 1) * LANES], preferred_element_type=F32
@@ -240,62 +255,82 @@
                 hid2[HALO : HALO + rows, :], gf, (((0,), (0,)), ((), ())), preferred_element_type=F32
             ))
             put(1, c, jnp.dot(gt[...], jnp.ones((rows, LANES), BF16), preferred_element_type=F32))
-        reps.append(send(grads.at[other, c], rep_in.at[c], rep_sem, (c,), {"rep": other}))
-
-    bats = []
-    for c in range(chunks):
+        reps[c] = send(grads.at[other, c], rep_in.at[c], rep_sem, (c,), {"rep": other})
+
+    bats, tms, gats, fins = {}, {}, {}, {}
+
+    def over_batch(c):
         reps[c].wait_recv()
         part_one[c] = (grads[r, c].astype(F32) + rep_in[c].astype(F32)).astype(BF16)
-        bats.append([
+        bats[c] = [
             send(part_one.at[c, lax.rem(b + o, n_batch)], batch_in.at[c, o - 1], batch_sem, (c, o - 1), batch_at(o))
             for o in range(1, n_batch)
-        ])
-    tms = []
-    for c in range(chunks):
+        ]
+
+    def over_tm(c):
         value = part_one[c, b].astype(F32)
         for o in range(1, n_batch):
             bats[c][o - 1].wait_recv()
             value += batch_in[c, o - 1].astype(F32)
         part_two[c] = value.astype(BF16)
-        tms.append([
+        tms[c] = [
             send(part_two.at[c, lax.rem(z + o, n_tm)], tm_in.at[c, o - 1], tm_sem, (c, o - 1), tm_at(o))
             for o in range(1, n_tm)
-        ])
-    gats = []
-    for c in range(chunks):
+        ]
+
+    def finish(c):
         value = part_two[c, z].astype(F32)
         for o in range(1, n_tm):
             tms[c][o - 1].wait_recv()
             value += tm_in[c, o - 1].astype(F32)
         final[r, c, b] = value.astype(BF16)
-        gats.append([
+        gats[c] = [
             send(final.at[r, c, b], final.at[r, c, b], gat_sem, (c, o - 1), batch_at(o)) for o in range(1, n_batch)
-        ])
-    fins = []
-    for c in range(chunks):
+        ]
+
+    def share_out(c):
         for copy in gats[c]:
             copy.wait_recv()
-        fins.append(send(final.at[r, c], final.at[r, c], fin_sem, (c,), {"rep": other}))
-    per_tap = channels // LANES
-    for c in range(chunks):
+        fins[c] = send(final.at[r, c], final.at[r, c], fin_sem, (c,), {"rep": other})
+
+    def write(c):
         fins[c].wait_recv()
         for owner in range(2):
+            sums_out[owner, c] = final[owner, c]
+
+    for c in range(chunks):
+        produce(c)
+        if c >= 1:
+            over_batch(c - 1)
+    over_batch(chunks - 1)
+    for step in range(chunks + 4):
+        for lag, stage in ((4, write), (3, share_out), (2, finish), (0, over_tm)):
+            if 0 <= step - lag < chunks:
+                stage(step - lag)
+    for copy in started:
+        copy.wait_send()
+
+
+def spread(emb_ref, sums_ref, emb_out, conv_out, bias_out, proj_out, tmp):
+    chunks, n_batch, piece = sums_ref.shape[1:4]
+    per_tap = conv_out.shape[1] // LANES
+    share = n_batch * piece
+    emb_out[...] = emb_ref[...]
+    for c in range(chunks):
+        for owner in range(2):
             if piece % 16 == 0:
-                value = final[owner, c].astype(F32).reshape(share, LANES)
+                value = sums_ref[owner, c].astype(F32).reshape(share, LANES)
             else:
                 for j in range(n_batch):
-                    tmp[j * piece : (j + 1) * piece, :] = final[owner, c, j].astype(F32)
-                value = tmp[0:share, :]
-            chunk = 2 * c + owner
+                    tmp[j * piece : (j + 1) * piece, :] = sums_ref[owner, c, j].astype(F32)
+                value = tmp[...]
             if c < chunks - 1:
-                k, part = divmod(chunk, per_tap)
+                k, part = divmod(2 * c + owner, per_tap)
                 conv_out[k, part * LANES : (part + 1) * LANES, :] = jnp.transpose(value)
             elif owner == 0:
                 proj_out[...] = value
             else:
                 bias_out[...] = jnp.transpose(value)[0:1, :]
-    for copy in started:
-        copy.wait_send()
 
 
 def per_device(
@@ -310,20 +345,17 @@
     piece = share // n_batch
     chunks = (3 * channels // LANES + 2) // 2
     vmem = pl.BlockSpec(memory_space=pltpu.VMEM)
-    smem = pl.BlockSpec(memory_space=pltpu.SMEM)
     hbm = pl.BlockSpec(memory_space=pl.ANY)
     nb = n_batch - 1
     dma = pltpu.SemaphoreType.DMA
-    embed, conv, bias, proj = pl.pallas_call(
+    embed, sums = pl.pallas_call(
         functools.partial(kernel, n_tm, n_batch, chunks),
         out_shape=(
             jax.ShapeDtypeStruct((rows, emb), BF16),
-            jax.ShapeDtypeStruct((3, channels, share), F32),
-            jax.ShapeDtypeStruct((1, share), F32),
-            jax.ShapeDtypeStruct((share, emb), F32),
+            jax.ShapeDtypeStruct((2, chunks, n_batch, piece, LANES), BF16),
         ),
-        in_specs=[smem, smem, vmem, vmem, vmem, hbm, vmem, hbm, vmem, vmem, vmem],
-        out_specs=(vmem, vmem, vmem, vmem),
+        in_specs=[vmem, vmem, vmem, vmem, vmem, hbm, vmem, hbm, vmem, vmem, vmem],
+        out_specs=(vmem, vmem),
         scratch_shapes=[
             pltpu.VMEM((3 * channels, channels), BF16),
             pltpu.VMEM((3 * channels, channels), BF16),
@@ -366,11 +398,23 @@
             collective_id=0, has_side_effects=True, vmem_limit_bytes=56 * 1024 * 1024
         ),
     )(
-        session_ids, counts, latents[0], session_gain, session_shift,
+        session_ids[None], counts, latents[0], session_gain, session_shift,
         first_conv_weight.reshape(3 * channels, channels), first_conv_bias[None],
         second_conv_weight.reshape(3 * channels, channels), second_conv_bias[None],
         proj_weight, offsets,
     )
+    embed, conv, bias, proj = pl.pallas_call(
+        spread,
+        out_shape=(
+            jax.ShapeDtypeStruct((rows, emb), BF16),
+            jax.ShapeDtypeStruct((3, channels, share), F32),
+            jax.ShapeDtypeStruct((1, share), F32),
+            jax.ShapeDtypeStruct((share, emb), F32),
+        ),
+        in_specs=[vmem, vmem],
+        out_specs=(vmem, vmem, vmem, vmem),
+        scratch_shapes=[pltpu.VMEM((share, LANES), F32)],
+    )(embed, sums)
     return embed[None], conv, bias[0], proj
 
 

time: 49.7 us -> 54.8 us (1.10)
  Pallas kernels: 42.7 us -> 52.7 us
  local copies, waits for them, and re-layouts: 4.81 us -> 0 us
    pallas_call x1, Pallas kernels: 42.7 us -> 50.5 us  [per_device(): pl.pallas_call(functools.partial(kernel, n_tm, n_batch, chunks), out_shap...]
    unnamed x8 -> x0, local copies, waits for them, and re-layouts: 4.81 us -> none
    pallas_call x0 -> x1, Pallas kernels: none -> 2.15 us  [per_device(): pl.pallas_call(spread, out_shape=(jax.ShapeDtypeStruct((rows, emb), BF16)...]
where the time goes in v2:
time: 54.8 us; the launch traced here: 54.6 us
  Pallas kernels  52.7 us (96%)
  between operations  1.93 us (4%)
    pallas_call x1, Pallas kernels, per_device(): pl.pallas_call(functools.partial(kernel, n_tm, n_batch, chunks), out_shap...  50.5 us
    pallas_call x1, Pallas kernels, per_device(): pl.pallas_call(spread, out_shape=(jax.ShapeDtypeStruct((rows, emb), BF16)...  2.15 us

profile of v2, /device:TPU:0, one launch (start us, length us, event | category | flops | bytes accessed | tf_op | source)
XLA Modules:
  0.0 54.6 jit_solution(17570570266116129003)
XLA Ops:
  1.9 50.5 %shard_map.138 = (bf16[512,128]{1,0:T(8,128)(2,1)}, bf16[2,7,2,64,128]{4,3,2,1,0:T(8,128)(2,1)}) custom-call(s32[1,1]{1,0:T(1,128)} %bitcast.8.ids_ref, s32[1,1]{1,0:T(1,128)S(6)} %copy.16.counts_ref, bf16[512,512]{1,0:T(8,128)(2,1)} %bitcast.11, f32[8,512]{1,0:T(8,128)} %gain_ref.1, f32[8,512]{1,0:T(8,128)} %shift_ref.1, bf16[1536,512]{1,0:T(8,128)(2,1)} %bitcast.9, ...), custom_call_target="tpu_custom_call" | custom-call | tf_op jit(solution)/shard_map/pallas_call | solution.py:351
  52.4 2.2 %shard_map.139 = (bf16[512,128]{1,0:T(8,128)(2,1)}, f32[3,512,128]{2,1,0:T(8,128)}, f32[1,128]{1,0:T(1,128)}, f32[128,128]{1,0:T(8,128)}) custom-call(bf16[512,128]{1,0:T(8,128)(2,1)} %get-tuple-element.10.emb_ref, bf16[2,7,2,64,128]{4,3,2,1,0:T(8,128)(2,1)} %get-tuple-element.11.sums_ref), custom_call_target="tpu_custom_call" | custom-call | tf_op jit(solution)/shard_map/pallas_call | solution.py:406

commit v3 on v2

--- a/solution.py
+++ b/solution.py
@@ -27,7 +27,7 @@
 
 def kernel(
     n_tm, n_batch, chunks,
-    ids_ref, counts_ref, lat_ref, gain_ref, shift_ref, w1_hbm, b1_ref, w2_hbm, b2_ref, proj_ref, off_ref,
+    id_count_ref, lat_ref, gain_ref, shift_ref, w1_hbm, b1_ref, w2_hbm, b2_ref, proj_ref, off_ref,
     emb_out, sums_out,
     w1, w2, wsem, halo, meta, meta_next, meta_pool, ext, taps, pre, slope, hid2, unit_s, scale_s, emb_ext, pool,
     xs, rhs, gt, grads, rep_in, part_one, batch_in, part_two, tm_in, final, tmp,
@@ -46,7 +46,7 @@
     load1.start()
     load2.start()
     meta[0:1, :] = off_ref[0:1, 0:LANES]
-    meta[1:2, :] = jnp.broadcast_to(counts_ref[...], (1, LANES))
+    meta[1:2, :] = id_count_ref[1:2, :]
     meta[2:8, :] = jnp.zeros((6, LANES), jnp.int32)
 
     barrier = pltpu.get_barrier_semaphore()
@@ -78,7 +78,7 @@
     nextm = send(meta, meta_next, meta_sem, (0,), tm_at(n_tm - 1))
     mpools = [send(meta, meta_pool.at[o - 1], mpool_sem, (o - 1,), batch_at(o)) for o in range(1, n_batch)]
 
-    pick = lax.broadcasted_iota(jnp.int32, gain_ref.shape, 0) == ids_ref[...]
+    pick = lax.broadcasted_iota(jnp.int32, gain_ref.shape, 0) == id_count_ref[0:1, 0:1]
     gain = jnp.sum(jnp.where(pick, gain_ref[...], 0.0), axis=0, keepdims=True)
     shift = jnp.sum(jnp.where(pick, shift_ref[...], 0.0), axis=0, keepdims=True)
 
@@ -303,10 +303,15 @@
         if c >= 1:
             over_batch(c - 1)
     over_batch(chunks - 1)
-    for step in range(chunks + 4):
-        for lag, stage in ((4, write), (3, share_out), (2, finish), (0, over_tm)):
-            if 0 <= step - lag < chunks:
-                stage(step - lag)
+    for step in range(chunks + 2):
+        if step < chunks:
+            over_tm(step)
+        if step >= 2:
+            finish(step - 2)
+    for c in range(chunks):
+        share_out(c)
+    for c in range(chunks):
+        write(c)
     for copy in started:
         copy.wait_send()
 
@@ -348,13 +353,16 @@
     hbm = pl.BlockSpec(memory_space=pl.ANY)
     nb = n_batch - 1
     dma = pltpu.SemaphoreType.DMA
+    id_count = jnp.where(
+        lax.broadcasted_iota(jnp.int32, (8, LANES), 0) == 0, session_ids[0], counts[0, 0]
+    )
     embed, sums = pl.pallas_call(
         functools.partial(kernel, n_tm, n_batch, chunks),
         out_shape=(
             jax.ShapeDtypeStruct((rows, emb), BF16),
             jax.ShapeDtypeStruct((2, chunks, n_batch, piece, LANES), BF16),
         ),
-        in_specs=[vmem, vmem, vmem, vmem, vmem, hbm, vmem, hbm, vmem, vmem, vmem],
+        in_specs=[vmem, vmem, vmem, vmem, hbm, vmem, hbm, vmem, vmem, vmem],
         out_specs=(vmem, vmem),
         scratch_shapes=[
             pltpu.VMEM((3 * channels, channels), BF16),
@@ -398,7 +406,7 @@
             collective_id=0, has_side_effects=True, vmem_limit_bytes=56 * 1024 * 1024
         ),
     )(
-        session_ids[None], counts, latents[0], session_gain, session_shift,
+        id_count, latents[0], session_gain, session_shift,
         first_conv_weight.reshape(3 * channels, channels), first_conv_bias[None],
         second_conv_weight.reshape(3 * channels, channels), second_conv_bias[None],
         proj_weight, offsets,

time: 54.8 us -> 46.6 us (0.85)
  Pallas kernels: 52.7 us -> 43.8 us
  local copies, waits for them, and re-layouts: 0 us -> 0.66 us
    pallas_call x1, Pallas kernels: 50.5 us -> 41.6 us  [per_device(): pl.pallas_call(functools.partial(kernel, n_tm, n_batch, chunks), out_shap...]
    iota x0 -> x1, local copies, waits for them, and re-layouts: none -> 0.66 us  [per_device(): lax.broadcasted_iota(jnp.int32, (8, LANES), 0) == 0]
where the time goes in v3:
time: 46.6 us; the launch traced here: 46.4 us
  Pallas kernels  43.8 us (94%)
  between operations  1.94 us (4%)
  local copies, waits for them, and re-layouts  0.66 us (1%)
    pallas_call x1, Pallas kernels, per_device(): pl.pallas_call(functools.partial(kernel, n_tm, n_batch, chunks), out_shap...  41.6 us
    pallas_call x1, Pallas kernels, per_device(): pl.pallas_call(spread, out_shape=(jax.ShapeDtypeStruct((rows, emb), BF16)...  2.15 us

profile of v3, /device:TPU:0, one launch (start us, length us, event | category | flops | bytes accessed | tf_op | source)
XLA Modules:
  0.0 46.4 jit_solution(2336337821780692135)
XLA Ops:
  1.9 0.7 %iota.7.id_count_ref = s32[8,128]{1,0:T(8,128)} broadcast(s32[8]{0:T(128)S(1)} %compare_select_fusion), dimensions={0} | broadcast | bytes 4128 | tf_op jit(solution)/shard_map/iota | solution.py:357
  2.6 41.6 %shard_map.138 = (bf16[512,128]{1,0:T(8,128)(2,1)}, bf16[2,7,2,64,128]{4,3,2,1,0:T(8,128)(2,1)}) custom-call(s32[8,128]{1,0:T(8,128)} %iota.7.id_count_ref, bf16[512,512]{1,0:T(8,128)(2,1)} %bitcast.13, f32[8,512]{1,0:T(8,128)} %gain_ref.1, f32[8,512]{1,0:T(8,128)} %shift_ref.1, bf16[1536,512]{1,0:T(8,128)(2,1)} %bitcast.11, f32[1,512]{1,0:T(1,128)} %bitcast.14, ...), custom_call_target="tpu_custom_call" | custom-call | tf_op jit(solution)/shard_map/pallas_call | solution.py:359
  44.2 2.2 %shard_map.139 = (bf16[512,128]{1,0:T(8,128)(2,1)}, f32[3,512,128]{2,1,0:T(8,128)}, f32[1,128]{1,0:T(1,128)}, f32[128,128]{1,0:T(8,128)}) custom-call(bf16[512,128]{1,0:T(8,128)(2,1)} %get-tuple-element.10.emb_ref, bf16[2,7,2,64,128]{4,3,2,1,0:T(8,128)(2,1)} %get-tuple-element.11.sums_ref), custom_call_target="tpu_custom_call" | custom-call | tf_op jit(solution)/shard_map/pallas_call | solution.py:414
  (1 shorter events, 0.0 us)

commit v4 on v3

--- a/solution.py
+++ b/solution.py
@@ -30,8 +30,8 @@
     id_count_ref, lat_ref, gain_ref, shift_ref, w1_hbm, b1_ref, w2_hbm, b2_ref, proj_ref, off_ref,
     emb_out, sums_out,
     w1, w2, wsem, halo, meta, meta_next, meta_pool, ext, taps, pre, slope, hid2, unit_s, scale_s, emb_ext, pool,
-    xs, rhs, gt, grads, rep_in, part_one, batch_in, part_two, tm_in, final, tmp,
-    halo_sem, meta_sem, mpool_sem, pool_sem, rep_sem, batch_sem, tm_sem, gat_sem, fin_sem,
+    xs, rhs, gt, grads, rep_in, part_one, batch_in, part_two, tm_in, final, tmp, zf_in, zf_sum, zf_batch,
+    halo_sem, meta_sem, mpool_sem, pool_sem, rep_sem, batch_sem, tm_sem, gat_sem, fin_sem, zf_sem, zf_batch_sem,
 ):
     rows, channels = lat_ref.shape
     total = rows + 2 * HALO
@@ -298,16 +298,50 @@
         for owner in range(2):
             sums_out[owner, c] = final[owner, c]
 
+    def tm_first(c):
+        reps[c].wait_recv()
+        part_one[c] = (grads[r, c].astype(F32) + rep_in[c].astype(F32)).astype(BF16)
+        tms[c] = [
+            send(part_one.at[c, :, lax.rem(z + o, n_tm)], zf_in.at[o - 1], zf_sem, (o - 1,), tm_at(o))
+            for o in range(1, n_tm)
+        ]
+
+    def then_batch(c):
+        value = part_one[c, :, z].astype(F32)
+        for o in range(1, n_tm):
+            tms[c][o - 1].wait_recv()
+            value += zf_in[o - 1].astype(F32)
+        zf_sum[...] = value.astype(BF16)
+        bats[c] = [
+            send(zf_sum.at[lax.rem(b + o, n_batch)], zf_batch.at[o - 1], zf_batch_sem, (o - 1,), batch_at(o))
+            for o in range(1, n_batch)
+        ]
+
+    def finish_tm_first(c):
+        value = zf_sum[b].astype(F32)
+        for o in range(1, n_batch):
+            bats[c][o - 1].wait_recv()
+            value += zf_batch[o - 1].astype(F32)
+        final[r, c, b] = value.astype(BF16)
+        gats[c] = [
+            send(final.at[r, c, b], final.at[r, c, b], gat_sem, (c, o - 1), batch_at(o)) for o in range(1, n_batch)
+        ]
+
     for c in range(chunks):
         produce(c)
-        if c >= 1:
+        if c == 1:
+            tm_first(0)
+        elif c > 1:
             over_batch(c - 1)
     over_batch(chunks - 1)
-    for step in range(chunks + 2):
+    over_tm(1)
+    over_tm(2)
+    then_batch(0)
+    for step in range(3, chunks + 2):
         if step < chunks:
             over_tm(step)
-        if step >= 2:
-            finish(step - 2)
+        finish(step - 2)
+    finish_tm_first(0)
     for c in range(chunks):
         share_out(c)
     for c in range(chunks):
@@ -392,6 +426,9 @@
             pltpu.VMEM((chunks, n_tm - 1, piece, LANES), BF16),
             pltpu.VMEM((2, chunks, n_batch, piece, LANES), BF16),
             pltpu.VMEM((channels, LANES), F32),
+            pltpu.VMEM((n_tm - 1, n_batch, piece, LANES), BF16),
+            pltpu.VMEM((n_batch, piece, LANES), BF16),
+            pltpu.VMEM((nb, piece, LANES), BF16),
             dma((2, 2)),
             dma((2, 1)),
             dma((2, nb)),
@@ -401,6 +438,8 @@
             dma((2, chunks, n_tm - 1)),
             dma((2, chunks, nb)),
             dma((2, chunks)),
+            dma((2, n_tm - 1)),
+            dma((2, nb)),
         ],
         compiler_params=pltpu.CompilerParams(
             collective_id=0, has_side_effects=True, vmem_limit_bytes=56 * 1024 * 1024

time: 46.6 us -> 46.2 us (level)
  no operation moved by 1% of the time
where the time goes in v4:
time: 46.2 us; the launch traced here: 46 us
  Pallas kernels  43.4 us (94%)
  between operations  1.94 us (4%)
  local copies, waits for them, and re-layouts  0.66 us (1%)
    pallas_call x1, Pallas kernels, per_device(): pl.pallas_call(functools.partial(kernel, n_tm, n_batch, chunks), out_shap...  41.3 us
    pallas_call x1, Pallas kernels, per_device(): pl.pallas_call(spread, out_shape=(jax.ShapeDtypeStruct((rows, emb), BF16)...  2.15 us

profile of v4, /device:TPU:0, one launch (start us, length us, event | category | flops | bytes accessed | tf_op | source)
XLA Modules:
  0.0 46.0 jit_solution(9771578787971743486)
XLA Ops:
  1.9 0.7 %iota.7.id_count_ref = s32[8,128]{1,0:T(8,128)} broadcast(s32[8]{0:T(128)S(1)} %compare_select_fusion), dimensions={0} | broadcast | bytes 4128 | tf_op jit(solution)/shard_map/iota | solution.py:391
  2.6 41.3 %shard_map.138 = (bf16[512,128]{1,0:T(8,128)(2,1)}, bf16[2,7,2,64,128]{4,3,2,1,0:T(8,128)(2,1)}) custom-call(s32[8,128]{1,0:T(8,128)} %iota.7.id_count_ref, bf16[512,512]{1,0:T(8,128)(2,1)} %bitcast.13, f32[8,512]{1,0:T(8,128)} %gain_ref.1, f32[8,512]{1,0:T(8,128)} %shift_ref.1, bf16[1536,512]{1,0:T(8,128)(2,1)} %bitcast.11, f32[1,512]{1,0:T(1,128)} %bitcast.14, ...), custom_call_target="tpu_custom_call" | custom-call | tf_op jit(solution)/shard_map/pallas_call | solution.py:393
  43.9 2.2 %shard_map.139 = (bf16[512,128]{1,0:T(8,128)(2,1)}, f32[3,512,128]{2,1,0:T(8,128)}, f32[1,128]{1,0:T(1,128)}, f32[128,128]{1,0:T(8,128)}) custom-call(bf16[512,128]{1,0:T(8,128)(2,1)} %get-tuple-element.10.emb_ref, bf16[2,7,2,64,128]{4,3,2,1,0:T(8,128)(2,1)} %get-tuple-element.11.sums_ref), custom_call_target="tpu_custom_call" | custom-call | tf_op jit(solution)/shard_map/pallas_call | solution.py:453
  (1 shorter events, 0.0 us)
